TPU v7x, 256 devices: a whole 4x4x8 slice. The times are simulated.
256 devices in a mesh: row: 16 (over y_lo, x, core), col: 16 (over y_hi, z).
Axes of the slice: x: 4, y: 4 (y_hi: 2, y_lo: 2; y = y_hi * 2 + y_lo), z: 8, core: 2. Of those that a mesh axis runs over, the one named last changes fastest.
Arguments:
- field: bfloat16 [64, 64, 32, 512], P('row', 'col'), may hold values from -6 to 6
- near_kernel: bfloat16 [9, 2, 2, 256, 256], replicated, may hold values from -0.09375 to 0.09375
- contact: int32 [64, 64, 9], P('row', 'col'), may hold values from 0 to 1
- pillar_shift: int32 [64, 64, 2], P('row', 'col'), may hold values from 0 to 15
- wave_index: int32 [2048, 2], replicated, may hold values from -32 to 31
- wave_form: bfloat16 [2048, 2, 256], replicated, may hold values from -0.25 to 0.25
- wave_weight: float32 [2048], replicated, may hold values from 0.5 to 4
Outputs:
- applied: float32 [64, 64, 32, 512], P('row', 'col')
All inputs are finite; a program needn't handle non-finite values.
Results may differ from a plain program's by a relative error of at most 0.0038.
Values may be sent and summed in bfloat16 or wider, within the bound.
A program may use at most 128 MiB of HBM per device.

v0:
```python
import math

import jax
import jax.numpy as jnp
from jax import lax
from jax.sharding import PartitionSpec as P

Q = 16


bloch_row = 0.3
bloch_col = 0.17


def extended(cells, sides, width):
    for axis, dim in sides:
        count = lax.axis_size(axis)
        head = lax.slice_in_dim(cells, 0, width, axis=dim)
        tail = lax.slice_in_dim(cells, cells.shape[dim] - width, cells.shape[dim], axis=dim)
        cells = jnp.concatenate(
            [
                lax.ppermute(tail, axis, [(i, (i + 1) % count) for i in range(count)]),
                cells,
                lax.ppermute(head, axis, [((i + 1) % count, i) for i in range(count)]),
            ],
            axis=dim,
        )
    return cells


def realify(real_part, imag_part):
    upper = jnp.concatenate([real_part.T, imag_part.T], axis=1)
    lower = jnp.concatenate([-imag_part.T, real_part.T], axis=1)
    return jnp.concatenate([upper, lower], axis=0)


def wave_angle(wave_index, fine_row, fine_col, row_mod, col_mod):
    order_row = wave_index[:, 0:1]
    order_col = wave_index[:, 1:2]
    turn_row = jnp.mod(order_row * fine_row[None, :], row_mod).astype(jnp.float32) / row_mod
    turn_col = jnp.mod(order_col * fine_col[None, :], col_mod).astype(jnp.float32) / col_mod
    drift = (
        bloch_row * fine_row.astype(jnp.float32) / row_mod
        + bloch_col * fine_col.astype(jnp.float32) / col_mod
    )
    return 2.0 * math.pi * (turn_row + turn_col + drift[None, :])


def local(field, near_kernel, contact, pillar_shift, wave_index, wave_form, wave_weight):
    rows_here = field.shape[0]
    cols_here = field.shape[1]
    sources = field.shape[2]
    width = field.shape[3]
    waves = wave_form.shape[0]
    n_row = lax.axis_size("row")
    n_col = lax.axis_size("col")
    rows_total = rows_here * n_row
    cols_total = cols_here * n_col
    row_mod = Q * rows_total
    col_mod = Q * cols_total
    wave_matrix = realify(wave_form[:, 0], wave_form[:, 1])
    padded = extended(field, (("row", 0), ("col", 1)), 1)
    global_row = lax.axis_index("row") * rows_here + jnp.arange(rows_here, dtype=jnp.int32)
    global_col = lax.axis_index("col") * cols_here + jnp.arange(cols_here, dtype=jnp.int32)
    fine_row = (Q * global_row[:, None] + pillar_shift[:, :, 0]).reshape(-1)
    fine_col = (Q * global_col[None, :] + pillar_shift[:, :, 1]).reshape(-1)
    angles = wave_angle(wave_index, fine_row, fine_col, row_mod, col_mod)
    cos_all = jnp.cos(angles).T
    sin_all = jnp.sin(angles).T
    projected = jnp.dot(field.reshape(-1, width), wave_matrix, preferred_element_type=jnp.float32)
    projected = projected.reshape(rows_here * cols_here, sources, 2, waves)
    hi = lax.Precision.HIGHEST
    coeff_real = jnp.einsum("pw,psw->sw", cos_all, projected[:, :, 0], precision=hi) - jnp.einsum(
        "pw,psw->sw", sin_all, projected[:, :, 1], precision=hi
    )
    coeff_imag = jnp.einsum("pw,psw->sw", cos_all, projected[:, :, 1], precision=hi) + jnp.einsum(
        "pw,psw->sw", sin_all, projected[:, :, 0], precision=hi
    )
    partial_coeff = jnp.stack([coeff_real, coeff_imag], axis=1)
    near = jnp.zeros((rows_here, cols_here, sources, width), jnp.float32)
    for offset in range(9):
        step_row = offset // 3 - 1
        step_col = offset % 3 - 1
        block = padded[
            1 + step_row : 1 + step_row + rows_here, 1 + step_col : 1 + step_col + cols_here
        ]
        block = block.reshape(-1, width)
        for variant in range(near_kernel.shape[1]):
            near_mat = realify(near_kernel[offset, variant, 0], near_kernel[offset, variant, 1])
            product = jnp.dot(block, near_mat, preferred_element_type=jnp.float32).reshape(
                rows_here, cols_here, sources, width
            )
            chosen = (contact[:, :, offset] == variant)[:, :, None, None]
            near = near + jnp.where(chosen, product, jnp.float32(0.0))
    far_scale = math.sqrt(width // 2 / (waves * rows_total * cols_total))
    owned = lax.psum_scatter(partial_coeff, ("row", "col"), scatter_dimension=2, tiled=True)
    owner = lax.axis_index("row") * n_col + lax.axis_index("col")
    count = owned.shape[2]
    scales = far_scale * lax.dynamic_slice_in_dim(wave_weight, owner * owned.shape[2], count, 0)
    weighted = (scales[None, None, :] * owned).astype(jnp.bfloat16)
    add_weighted = lax.all_gather(weighted, ("row", "col"), axis=2, tiled=True)
    count = add_weighted.shape[2]
    cos_part = cos_all[:, None, :]
    sin_part = sin_all[:, None, :]
    weight_real = add_weighted[:, 0].astype(jnp.float32)[None]
    weight_imag = add_weighted[:, 1].astype(jnp.float32)[None]
    spread_real = cos_part * weight_real + sin_part * weight_imag
    spread_imag = cos_part * weight_imag - sin_part * weight_real
    spread = (
        jnp.concatenate([spread_real, spread_imag], axis=-1)
        .astype(jnp.bfloat16)
        .reshape(-1, 2 * count)
    )
    columns = jnp.concatenate(
        [
            lax.slice_in_dim(wave_matrix, 0, count, axis=1),
            lax.dynamic_slice_in_dim(wave_matrix, waves, count, 1),
        ],
        axis=1,
    )
    far = lax.dot_general(
        spread, columns, (((1,), (1,)), ((), ())), preferred_element_type=jnp.float32
    )
    return near + far.reshape(rows_here, cols_here, sources, width)


def solution(mesh):
    placed = (
        P("row", "col", None, None),
        P(),
        P("row", "col", None),
        P("row", "col", None),
        P(),
        P(),
        P(),
    )
    return jax.shard_map(
        local, mesh=mesh, in_specs=placed, out_specs=P("row", "col", None, None), check_vma=False
    )
```

profile of v0, /device:TPU:0, one launch (start us, length us, event | category | flops | bytes accessed | tf_op | source)
XLA Modules:
  0.0 1004.8 jit_solution(13671285341603411900)
XLA Ops:
  6.5 6.5 fusion.183
  13.0 5.8 copy.195
  18.8 2.6 copy.196
  22.5 7.4 convolution_bitcast_fusion
  29.9 8.9 copy.148
  38.8 11.8 %reshape.487 = f32[16,32,2,2048]{3,2,1,0:T(2,128)} reshape(f32[512,4096]{1,0:T(8,128)} %copy.148) | data formatting | bytes 16777216 | tf_op jit(solution)/shard_map/reshape | solution.py:71
  50.6 12.1 %fusion.180 = (f32[16,32,1,2048]{3,2,1,0:T(1,128)}, f32[16,32,1,2048]{3,2,1,0:T(1,128)}) fusion(f32[16,32,2,2048]{3,2,1,0:T(2,128)} %reshape.487), kind=kLoop, calls=%fused_computation.305 | loop fusion | bytes 16777216 | tf_op jit(solution)/shard_map/slice | solution.py:74
  64.9 6.9 fusion.6
  72.0 2.2 copy.149
  75.0 3.9 collective-permute-start.1
  78.9 2.7 fusion.181
  81.6 3.0 fusion.182
  84.6 1.7 fusion.178
  86.3 1.7 copy.228
  87.9 1.6 bitcast_negate_fusion.1
  89.5 1.7 copy.226
  91.2 1.6 bitcast_negate_fusion.2
  92.7 1.7 copy.224
  94.4 1.6 bitcast_negate_fusion.3
  95.9 1.7 copy.222
  97.6 1.6 bitcast_negate_fusion.4
  99.2 1.7 copy.220
  100.8 1.6 bitcast_negate_fusion.5
  102.4 1.7 copy.218
  104.1 1.6 bitcast_negate_fusion.6
  105.6 1.7 copy.216
  107.3 1.5 bitcast_negate_fusion.7
  109.6 1.6 bitcast_negate_fusion.9
  115.4 1.7 copy.204
  117.1 1.6 bitcast_negate_fusion.13
  118.6 1.6 copy.202
  120.3 1.6 bitcast_negate_fusion.14
  121.8 1.7 copy.200
  123.5 1.6 bitcast_negate_fusion.15
  127.6 2.0 fusion.156
  129.6 2.6 fusion.83
  132.2 2.6 fusion.75
  142.3 1.7 copy.207
  143.9 1.7 copy.205
  145.6 1.7 copy.203
  147.2 1.7 copy.201
  149.0 1.7 copy.199
  152.1 1.9 compare_reduce_fusion.7
  156.9 6.8 collective-permute-start.3
  163.7 2.4 convolution_select_fusion
  166.1 2.5 convolution_select_fusion.1
  168.6 1.5 convolution_select_fusion.2
  170.1 1.4 convolution_select_fusion.3
  171.6 165.6 %all-reduce.3.cloned.1.call-done = f32[32,2,2048]{0,1,2:T(2,128)} async-done(((f32[32,2,2048]{0,1,2:T(2,128)}), f32[32,2,2048]{0,1,2:T(2,128)}) %all-reduce.3.cloned.1.call-update) | async-done | bytes 524304
  337.9 630.5 %all_gather.3 = bf16[32,2,2048]{0,1,2:T(2,128)(2,1)S(1)} all-gather(bf16[32,2,8]{0,1,2:T(2,128)(2,1)S(1)} %fusion.157), channel_id=1, replica_groups=mesh['row'=16,'col'=16] {'row','col'}, dimensions={2}, use_global_device_ids=true | all-gather | bytes 263168 | tf_op jit(solution)/shard_map/all_gather | solution.py:101
  968.4 2.2 slice_convert_fusion.1
  970.6 1.5 copy.151
  973.2 2.5 add_convert_fusion
  975.7 2.4 fusion
  978.2 1.5 convolution_select_fusion.4
  979.8 1.4 convolution_select_fusion.5
  981.3 1.4 convolution_select_fusion.6
  982.8 1.4 convolution_select_fusion.7
  984.3 1.4 convolution_select_fusion.8
  987.3 1.4 convolution_select_fusion.11
  988.8 1.4 convolution_select_fusion.12
  990.3 1.5 convolution_select_fusion.13
  993.3 1.9 fusion.26
  995.2 2.7 fusion.25
  (196 shorter events, 28.3 us)
Async XLA Ops:
  6.5 330.6 %all-reduce.3.cloned.1.call-start = ((), (), s32[]{:S(2)}) async-start(), calls=%async_computation | async-start | bytes 4194304
  50.6 12.7 %copy-start.57 = (s32[4,4,2]{1,2,0:T(2,128)S(1)}, s32[4,4,2]{1,2,0:T(2,128)}, u32[]{:S(2)}) copy-start(s32[4,4,2]{1,2,0:T(2,128)} %param.10) | copy-start | bytes 388
  50.6 13.6 %copy-start.56 = (s32[2048,2]{0,1:T(2,128)S(1)}, s32[2048,2]{0,1:T(2,128)}, u32[]{:S(2)}) copy-start(s32[2048,2]{0,1:T(2,128)} %param.11) | copy-start | bytes 49156
  64.1 7.8 copy-start.59
  75.0 79.0 %collective-permute-start = (bf16[1,4,32,512]{3,2,1,0:T(8,128)(2,1)}, bf16[1,4,32,512]{3,2,1,0:T(8,128)(2,1)}, u32[]{:S(2)}, u32[]{:S(2)}) collective-permute-start(bf16[1,4,32,512]{3,2,1,0:T(8,128)(2,1)} %get-tuple-element.89), channel_id=1, source_target_pairs={{0,16},{16,32},{32,48},{48,64},{64,80},{80,96},{96,112},{112,128},... | collective-permute-start | bytes 393224 | tf_op jit(solution)/shard_map/ppermute | solution.py:22
  75.0 80.1 %collective-permute-start.1 = (bf16[1,4,32,512]{3,2,1,0:T(8,128)(2,1)}, bf16[1,4,32,512]{3,2,1,0:T(8,128)(2,1)}, u32[]{:S(2)}, u32[]{:S(2)}) collective-permute-start(bf16[1,4,32,512]{3,2,1,0:T(8,128)(2,1)} %get-tuple-element.88), channel_id=1, source_target_pairs={{16,0},{32,16},{48,32},{64,48},{80,64},{96,80},{112,96},{128,112},... | collective-permute-start | bytes 393224 | tf_op jit(solution)/shard_map/ppermute | solution.py:24
  111.2 13.8 %copy-start.18 = (bf16[1,1,1,256,256]{3,4,2,1,0:T(8,128)(2,1)}, bf16[1,1,1,256,256]{3,4,2,1,0:T(8,128)(2,1)S(1)}, u32[]{:S(2)}) copy-start(bf16[1,1,1,256,256]{3,4,2,1,0:T(8,128)(2,1)S(1)} %copy.210) | copy-start | bytes 393220
  114.7 12.1 %copy-start.14 = (bf16[1,1,1,256,256]{3,4,2,1,0:T(8,128)(2,1)}, bf16[1,1,1,256,256]{3,4,2,1,0:T(8,128)(2,1)S(1)}, u32[]{:S(2)}) copy-start(bf16[1,1,1,256,256]{3,4,2,1,0:T(8,128)(2,1)S(1)} %copy.206) | copy-start | bytes 393220
  132.2 20.0 %copy-start.10 = (s32[4,4,9]{2,1,0:T(4,128)S(1)}, s32[4,4,9]{2,1,0:T(4,128)}, u32[]{:S(2)}) copy-start(s32[4,4,9]{2,1,0:T(4,128)} %param.9) | copy-start | bytes 1732
  140.8 22.9 %copy-start.53 = (bf16[1,1,1,256,256]{3,4,2,1,0:T(8,128)(2,1)S(1)}, bf16[1,1,1,256,256]{3,4,2,1,0:T(8,128)(2,1)}, u32[]{:S(2)}) copy-start(bf16[1,1,1,256,256]{3,4,2,1,0:T(8,128)(2,1)} %copy.223) | copy-start | bytes 393220
  147.2 18.9 %copy-start.27 = (bf16[1,1,1,256,256]{3,4,2,1,0:T(8,128)(2,1)S(1)}, bf16[1,1,1,256,256]{3,4,2,1,0:T(8,128)(2,1)}, u32[]{:S(2)}) copy-start(bf16[1,1,1,256,256]{3,4,2,1,0:T(8,128)(2,1)} %copy.222) | copy-start | bytes 393220
  147.2 18.9 %copy-start.44 = (bf16[256,256]{1,0:T(8,128)(2,1)S(1)}, bf16[256,256]{1,0:T(8,128)(2,1)}, u32[]{:S(2)}) copy-start(bf16[256,256]{1,0:T(8,128)(2,1)} %bitcast_negate_fusion.4) | copy-start | bytes 393220
  155.1 13.5 %copy-start.29 = (bf16[1,1,1,256,256]{3,4,2,1,0:T(8,128)(2,1)S(1)}, bf16[1,1,1,256,256]{3,4,2,1,0:T(8,128)(2,1)}, u32[]{:S(2)}) copy-start(bf16[1,1,1,256,256]{3,4,2,1,0:T(8,128)(2,1)} %copy.204) | copy-start | bytes 393220
  155.1 13.5 %copy-start.52 = (bf16[256,256]{1,0:T(8,128)(2,1)S(1)}, bf16[256,256]{1,0:T(8,128)(2,1)}, u32[]{:S(2)}) copy-start(bf16[256,256]{1,0:T(8,128)(2,1)} %bitcast_negate_fusion.13) | copy-start | bytes 393220
  155.2 13.5 %copy-start.55 = (bf16[1,1,1,256,256]{3,4,2,1,0:T(8,128)(2,1)S(1)}, bf16[1,1,1,256,256]{3,4,2,1,0:T(8,128)(2,1)}, u32[]{:S(2)}) copy-start(bf16[1,1,1,256,256]{3,4,2,1,0:T(8,128)(2,1)} %copy.203) | copy-start | bytes 393220
  156.9 821.2 %collective-permute-start.3 = (bf16[6,1,32,512]{3,2,1,0:T(8,128)(2,1)}, bf16[6,1,32,512]{3,2,1,0:T(8,128)(2,1)}, u32[]{:S(2)}, u32[]{:S(2)}) collective-permute-start(bf16[6,1,32,512]{3,2,1,0:T(8,128)(2,1)} %get-tuple-element.82), channel_id=1, source_target_pairs={{1,0},{2,1},{3,2},{4,3},{5,4},{6,5},{7,6},{8,7},{9,8},{10,9},{11,1... | collective-permute-start | bytes 589832 | tf_op jit(solution)/shard_map/ppermute | solution.py:24
  163.7 817.5 %collective-permute-start.2 = (bf16[6,1,32,512]{3,2,1,0:T(8,128)(2,1)}, bf16[6,1,32,512]{3,2,1,0:T(8,128)(2,1)}, u32[]{:S(2)}, u32[]{:S(2)}) collective-permute-start(bf16[6,1,32,512]{3,2,1,0:T(8,128)(2,1)} %get-tuple-element.81), channel_id=1, source_target_pairs={{0,1},{1,2},{2,3},{3,4},{4,5},{5,6},{6,7},{7,8},{8,9},{9,10},{10,1... | collective-permute-start | bytes 589832 | tf_op jit(solution)/shard_map/ppermute | solution.py:22
  166.1 4.0 copy-start.28
  166.1 4.0 copy-start.50
  166.1 4.0 copy-start.54
  973.2 2.5 copy-start.1
  973.2 2.5 copy-start.9
  975.7 2.5 copy-start.26
  975.7 2.5 copy-start.39
  975.7 2.5 copy-start.51
  975.7 2.5 copy-start.69
  978.2 3.0 copy-start.25
  978.2 3.0 copy-start.38
  978.2 3.0 copy-start.48
  978.2 3.0 copy-start.67
  979.8 3.0 copy-start.23
  979.8 3.0 copy-start.36
  979.8 3.0 copy-start.47
  979.8 3.0 copy-start.66
  981.3 3.0 copy-start.22
  981.3 3.0 copy-start.35
  981.3 3.0 copy-start.46
  981.3 3.0 copy-start.65
  982.8 3.0 copy-start.21
  982.8 3.0 copy-start.34
  982.8 3.0 copy-start.45
  982.8 3.0 copy-start.64
  984.3 3.0 copy-start.19
  984.3 3.0 copy-start.32
  984.3 3.0 copy-start.43
  984.3 3.0 copy-start.63
  985.8 3.0 copy-start.17
  985.8 3.0 copy-start.31
  985.8 3.0 copy-start.42
  985.8 3.0 copy-start.62
  987.3 3.0 copy-start.15
  987.3 3.0 copy-start.30
  987.3 3.0 copy-start.40
  987.3 3.0 copy-start.61
  988.8 3.1 copy-start.20
  988.8 3.1 copy-start.33
  988.8 3.1 copy-start.41
  988.8 3.1 copy-start.60
  990.2 3.0 copy-start.2
  990.3 3.0 copy-start.3
  990.3 3.0 copy-start.6
  990.3 3.0 copy-start.7
  990.3 3.0 copy-start.11
  990.3 3.0 copy-start.13
  (11 other events, 17.0 us)
Sparse Core Ops, SparseCore 0:
  74.4 262.6 all-reduce.2
where the time goes:
time: 1010 us; the launch traced here: 1000 us
  blocking collectives  630 us (62%)
  waiting for transfers between devices  166 us (16%)
  local copies, waits for them, and re-layouts  102 us (10%)
  matrix products  41.5 us (4%)
  other arithmetic  40.3 us (4%)
  between operations  14.6 us (1%)
  starting transfers between devices  10.6 us (1%)
    all_gather x1, blocking collectives, local(): add_weighted = lax.all_gather(weighted, ('row', 'col'), axis=2, tiled=True)  630 us
    unnamed x2, waiting for transfers between devices  166 us
    unnamed x175, local copies, waits for them, and re-layouts  48.2 us
    dot_general x18, matrix products, local(): jnp.dot(block, near_mat, preferred_element_type=jnp.float32)  31.8 us
    neg x18, other arithmetic, realify(): lower = jnp.concatenate([-imag_part.T, real_part.T], axis=1)  21.7 us
  transfers between devices with their start and end apart: 5, of which 1 were waited for; matrix products, arithmetic and copies ran while one was open for 10% of the time, Pallas kernels for 0%

commit v1 on v0

v1 whole, which is shorter than its diff:
```python
import functools
import math

import jax
import jax.numpy as jnp
from jax import lax
from jax.experimental import pallas as pl
from jax.experimental.pallas import tpu as pltpu
from jax.sharding import PartitionSpec as P

Q = 16
LANES = 128
BLOCH_ROW = 0.3
BLOCH_COL = 0.17
MESH = pl.DeviceIdType.MESH
NT = (((1,), (1,)), ((), ()))

PARTIAL = jnp.float32
NEAR_SPLIT = (0, 3, 5, 7, 9)


def turn_to_cos_sin(turn):
    quarter = jnp.round(turn * 4.0)
    angle = (turn - quarter * 0.25) * (2.0 * math.pi)
    square = angle * angle
    sine = angle * (
        1.0
        + square
        * (-1.0 / 6 + square * (1.0 / 120 + square * (-1.0 / 5040 + square * (1.0 / 362880))))
    )
    cosine = 1.0 + square * (
        -0.5
        + square
        * (1.0 / 24 + square * (-1.0 / 720 + square * (1.0 / 40320 + square * (-1.0 / 3628800))))
    )
    which = quarter.astype(jnp.int32) & 3
    odd = (which & 1) == 1
    c = jnp.where(odd, sine, cosine)
    s = jnp.where(odd, cosine, sine)
    c = jnp.where((which == 1) | (which == 2), -c, c)
    s = jnp.where(which >= 2, -s, s)
    return c, s


def kernel(
    dims,
    field,
    near_kernel,
    contact,
    shift,
    wave_index,
    wave_form,
    wave_weight,
    out,
    xpad,
    form,
    by_wave,
    by_chunk,
    near_mats,
    x2,
    lhs,
    acc,
    cos_all,
    sin_all,
    send1,
    recv1,
    total1,
    send2,
    recv2,
    total2,
    waves_in,
    waves_now,
    local_sem,
    halo_send,
    halo_recv,
    s1,
    r1,
    s2,
    r2,
    s3,
    r3,
    s4,
    r4,
):
    n_row, n_col, rows, cols, sources, waves, unknowns = dims
    pillars = rows * cols
    own = 2 * sources // n_col
    pairs = n_row // 2
    me_row, me_col = lax.axis_index("row"), lax.axis_index("col")
    row_mod, col_mod = Q * rows * n_row, Q * cols * n_col

    def at(row_step, col_step):
        return (lax.rem(me_row + row_step + n_row, n_row), lax.rem(me_col + col_step + n_col, n_col))

    loads = [
        pltpu.make_async_copy(field, xpad.at[1 : rows + 1, 1 : cols + 1], local_sem.at[0]),
        pltpu.make_async_copy(wave_form, form, local_sem.at[1]),
    ]
    for variant in range(2):
        for part in range(2):
            which = 2 * variant + part
            loads.append(
                pltpu.make_async_copy(
                    near_kernel.at[:, variant, part],
                    near_mats.at[:, :, which * unknowns : (which + 1) * unknowns],
                    local_sem.at[2 + which],
                )
            )
    for load in loads:
        load.start()

    barrier = pltpu.get_barrier_semaphore()

    def greet_row(step, _):
        pl.semaphore_signal(
            barrier, inc=1, device_id=(lax.rem(me_row + step, n_row), me_col), device_id_type=MESH
        )
        return 0

    def greet_col(step, _):
        pl.semaphore_signal(
            barrier, inc=1, device_id=(me_row, lax.rem(me_col + step, n_col)), device_id_type=MESH
        )
        return 0

    lax.fori_loop(1, n_row, greet_row, 0)
    lax.fori_loop(1, n_col, greet_col, 0)
    for row_step in (-1, 1):
        for col_step in (-1, 1):
            pl.semaphore_signal(
                barrier, inc=1, device_id=at(row_step, col_step), device_id_type=MESH
            )

    down = lax.broadcasted_iota(jnp.int32, (pillars, LANES), 0)
    fine_row = jnp.zeros((pillars, LANES), jnp.int32)
    fine_col = jnp.zeros((pillars, LANES), jnp.int32)
    for p in range(pillars):
        r, c = divmod(p, cols)
        fine_row = jnp.where(down == p, Q * (me_row * rows + r) + shift[r, 0, c], fine_row)
        fine_col = jnp.where(down == p, Q * (me_col * cols + c) + shift[r, 1, c], fine_col)
    drift = (BLOCH_ROW / row_mod) * fine_row.astype(jnp.float32) + (
        BLOCH_COL / col_mod
    ) * fine_col.astype(jnp.float32)

    def phases(j, _):
        here = pl.ds(pl.multiple_of(j * LANES, LANES), LANES)
        m = wave_index[0:1, here]
        n = wave_index[1:2, here]
        turn_row = ((m * fine_row) & (row_mod - 1)).astype(jnp.float32) * (1.0 / row_mod)
        turn_col = ((n * fine_col) & (col_mod - 1)).astype(jnp.float32) * (1.0 / col_mod)
        c, s = turn_to_cos_sin(turn_row + turn_col + drift)
        cos_all[:, here] = c
        sin_all[:, here] = s
        return 0

    lax.fori_loop(0, waves // LANES, phases, 0)

    to = lax.broadcasted_iota(jnp.int32, (2 * LANES, 2 * LANES), 0)
    source = lax.broadcasted_iota(jnp.int32, (2 * LANES, 2 * LANES), 1)
    wanted = jnp.where(to < LANES, 2 * to, 2 * (to - LANES) + 1)
    apart = jnp.where(source == wanted, 1.0, 0.0).astype(jnp.bfloat16)
    loads[1].wait()

    def split(chunk, _):
        for half in range(2):
            first = pl.multiple_of((2 * chunk + half) * LANES, LANES)
            block = form[pl.ds(first, LANES)].reshape(2 * LANES, unknowns)
            rows_apart = jnp.dot(apart, block, preferred_element_type=jnp.float32)
            rows_apart = rows_apart.astype(jnp.bfloat16)
            by_wave[pl.ds(first, LANES), 0:unknowns] = rows_apart[:LANES]
            by_wave[pl.ds(first, LANES), unknowns : 2 * unknowns] = rows_apart[LANES:]
            by_chunk[chunk, half * LANES : (half + 1) * LANES] = rows_apart[:LANES]
            by_chunk[chunk, (2 + half) * LANES : (3 + half) * LANES] = rows_apart[LANES:]
        return 0

    lax.fori_loop(0, pairs, split, 0)

    loads[0].wait()
    for p in range(pillars):
        r, c = divmod(p, cols)
        x = xpad[1 + r, 1 + c]
        real, imag = x[:, :unknowns], x[:, unknowns:]
        base = 2 * sources * p
        x2[base : base + sources, :unknowns] = real
        x2[base : base + sources, unknowns:] = -imag
        x2[base + sources : base + 2 * sources, :unknowns] = imag
        x2[base + sources : base + 2 * sources, unknowns:] = real

    pl.semaphore_wait(barrier, (n_row - 1) + (n_col - 1) + 4)

    halos = []
    spans = {-1: (slice(0, 1), rows + 1), 1: (slice(rows - 1, rows), 0)}
    col_spans = {-1: (slice(0, 1), cols + 1), 1: (slice(cols - 1, cols), 0)}
    for row_step in (-1, 0, 1):
        for col_step in (-1, 0, 1):
            if (row_step, col_step) == (0, 0):
                continue
            if row_step:
                from_row, into = spans[row_step]
                to_row = slice(into, into + 1)
            else:
                from_row, to_row = slice(0, rows), slice(1, rows + 1)
            if col_step:
                from_col, into = col_spans[col_step]
                to_col = slice(into, into + 1)
            else:
                from_col, to_col = slice(0, cols), slice(1, cols + 1)
            k = len(halos)
            halos.append(
                pltpu.make_async_remote_copy(
                    src_ref=field.at[from_row, from_col],
                    dst_ref=xpad.at[to_row, to_col],
                    send_sem=halo_send.at[k],
                    recv_sem=halo_recv.at[k],
                    device_id=at(row_step, col_step),
                    device_id_type=MESH,
                )
            )
    for halo in halos:
        halo.start()

    def first_copy(peer, slot):
        return pltpu.make_async_remote_copy(
            src_ref=send1.at[peer],
            dst_ref=recv1.at[slot],
            send_sem=s1.at[peer],
            recv_sem=r1.at[slot],
            device_id=(peer, me_col),
            device_id_type=MESH,
        )

    my_pair = lax.div(me_row, 2)

    def project(step, _):
        pair = lax.rem(my_pair + 1 + step, pairs)
        first = pl.multiple_of(pair * 2 * LANES, 2 * LANES)
        projected = lax.dot_general(
            x2[...],
            by_wave[pl.ds(first, 2 * LANES), :],
            NT,
            preferred_element_type=jnp.float32,
        )
        for half in range(2):
            here = pl.ds(pl.multiple_of(first + half * LANES, LANES), LANES)
            lanes = slice(half * LANES, (half + 1) * LANES)
            real = jnp.zeros((sources, LANES), jnp.float32)
            imag = jnp.zeros((sources, LANES), jnp.float32)
            for p in range(pillars):
                base = 2 * sources * p
                pr = projected[base : base + sources, lanes]
                pi = projected[base + sources : base + 2 * sources, lanes]
                c = cos_all[p : p + 1, here]
                s = sin_all[p : p + 1, here]
                real = real + (c * pr - s * pi)
                imag = imag + (c * pi + s * pr)
            peer = 2 * pair + half
            send1[peer, 0:sources] = real.astype(send1.dtype)
            send1[peer, sources : 2 * sources] = imag.astype(send1.dtype)

            @pl.when(peer != me_row)
            def _():
                first_copy(peer, me_row).start()

        return 0

    lax.fori_loop(0, pairs, project, 0)

    def near_offset(offset, _):
        a = lax.div(offset, 3)
        b = lax.rem(offset, 3)
        for p in range(pillars):
            r, c = divmod(p, cols)
            x = xpad[r + a, c + b]
            real, imag = x[:, :unknowns], x[:, unknowns:]
            base = 2 * sources * p
            for variant in range(2):
                mask = jnp.where(contact[r, c, offset] == variant, 1.0, 0.0)
                mask = jnp.full((sources, unknowns), mask, jnp.float32).astype(jnp.bfloat16)
                chosen_real, chosen_imag = real * mask, imag * mask
                low = 2 * variant * unknowns
                mid, high = low + unknowns, low + 2 * unknowns
                lhs[base : base + sources, low:mid] = chosen_real
                lhs[base : base + sources, mid:high] = -chosen_imag
                lhs[base + sources : base + 2 * sources, low:mid] = chosen_imag
                lhs[base + sources : base + 2 * sources, mid:high] = chosen_real
        acc[...] += lax.dot_general(
            lhs[...], near_mats[offset], NT, preferred_element_type=jnp.float32
        )
        return 0

    for load in loads[2:]:
        load.wait()
    for halo in halos:
        halo.wait_recv()
    acc[...] = jnp.zeros_like(acc)
    lax.fori_loop(NEAR_SPLIT[0], NEAR_SPLIT[1], near_offset, 0)

    total1[...] = send1[me_row].astype(jnp.float32)

    def gather1(step, _):
        peer = lax.rem(me_row + step, n_row)
        first_copy(peer, peer).wait_recv()
        total1[...] += recv1[peer].astype(jnp.float32)
        return 0

    lax.fori_loop(1, n_row, gather1, 0)
    for k in range(n_col):
        send2[k] = total1[k * own : (k + 1) * own]

    def second_copy(peer, slot):
        return pltpu.make_async_remote_copy(
            src_ref=send2.at[peer],
            dst_ref=recv2.at[slot],
            send_sem=s2.at[peer],
            recv_sem=r2.at[slot],
            device_id=(me_row, peer),
            device_id_type=MESH,
        )

    def spread2(step, _):
        peer = lax.rem(me_col + step, n_col)
        second_copy(peer, me_col).start()
        return 0

    lax.fori_loop(1, n_col, spread2, 0)
    lax.fori_loop(NEAR_SPLIT[1], NEAR_SPLIT[2], near_offset, 0)

    total2[...] = send2[me_col]

    def gather2(step, _):
        peer = lax.rem(me_col + step, n_col)
        second_copy(peer, peer).wait_recv()
        total2[...] += recv2[peer]
        return 0

    lax.fori_loop(1, n_col, gather2, 0)
    far_scale = math.sqrt(unknowns / (waves * rows * n_row * cols * n_col))
    scale = far_scale * wave_weight[pl.ds(me_row, 1), :]
    waves_in[me_row, me_col] = (scale * total2[...]).astype(jnp.bfloat16)

    def third_copy(peer, slot):
        return pltpu.make_async_remote_copy(
            src_ref=waves_in.at[me_row, me_col],
            dst_ref=waves_in.at[me_row, slot],
            send_sem=s3.at[peer],
            recv_sem=r3.at[slot],
            device_id=(me_row, peer),
            device_id_type=MESH,
        )

    def spread3(step, _):
        peer = lax.rem(me_col + step, n_col)
        third_copy(peer, me_col).start()
        return 0

    lax.fori_loop(1, n_col, spread3, 0)
    lax.fori_loop(NEAR_SPLIT[2], NEAR_SPLIT[3], near_offset, 0)

    def gather3(step, _):
        peer = lax.rem(me_col + step, n_col)
        third_copy(peer, peer).wait_recv()
        return 0

    lax.fori_loop(1, n_col, gather3, 0)

    def fourth_copy(peer, slot):
        return pltpu.make_async_remote_copy(
            src_ref=waves_in.at[me_row],
            dst_ref=waves_in.at[slot],
            send_sem=s4.at[peer],
            recv_sem=r4.at[slot],
            device_id=(peer, me_col),
            device_id_type=MESH,
        )

    def spread4(step, _):
        peer = lax.rem(me_row + step, n_row)
        fourth_copy(peer, me_row).start()
        return 0

    lax.fori_loop(1, n_row, spread4, 0)
    lax.fori_loop(NEAR_SPLIT[3], NEAR_SPLIT[4], near_offset, 0)

    def far_pair(step, _):
        pair = lax.rem(my_pair + step, pairs)
        for half in range(2):
            peer = 2 * pair + half

            @pl.when(peer != me_row)
            def _():
                fourth_copy(peer, peer).wait_recv()

            for k in range(n_col):
                waves_now[half, k * own : (k + 1) * own] = waves_in[peer, k].astype(jnp.float32)
            here = pl.ds(pl.multiple_of((2 * pair + half) * LANES, LANES), LANES)
            wr = waves_now[half, 0:sources]
            wi = waves_now[half, sources : 2 * sources]
            low = slice(half * LANES, (half + 1) * LANES)
            high = slice((2 + half) * LANES, (3 + half) * LANES)
            for p in range(pillars):
                base = 2 * sources * p
                c = cos_all[p : p + 1, here]
                s = sin_all[p : p + 1, here]
                sr = (c * wr + s * wi).astype(jnp.bfloat16)
                si = (c * wi - s * wr).astype(jnp.bfloat16)
                x2[base : base + sources, low] = sr
                x2[base : base + sources, high] = si
                x2[base + sources : base + 2 * sources, low] = si
                x2[base + sources : base + 2 * sources, high] = -sr
        acc[...] += jnp.dot(x2[...], by_chunk[pair], preferred_element_type=jnp.float32)
        return 0

    lax.fori_loop(0, pairs, far_pair, 0)
    for p in range(pillars):
        r, c = divmod(p, cols)
        base = 2 * sources * p
        out[r, c, :, :unknowns] = acc[base : base + sources]
        out[r, c, :, unknowns:] = acc[base + sources : base + 2 * sources]

    for halo in halos:
        halo.wait_send()

    def drain_row(step, _):
        peer = lax.rem(me_row + step, n_row)
        first_copy(peer, me_row).wait_send()
        fourth_copy(peer, me_row).wait_send()
        return 0

    def drain_col(step, _):
        peer = lax.rem(me_col + step, n_col)
        second_copy(peer, me_col).wait_send()
        third_copy(peer, me_col).wait_send()
        return 0

    lax.fori_loop(1, n_row, drain_row, 0)
    lax.fori_loop(1, n_col, drain_col, 0)


def local(field, near_kernel, contact, pillar_shift, wave_index, wave_form, wave_weight):
    rows, cols, sources, width = field.shape
    waves = wave_form.shape[0]
    unknowns = width // 2
    n_row = lax.axis_size("row")
    n_col = lax.axis_size("col")
    own = 2 * sources // n_col
    pillars = rows * cols
    stacked = 2 * pillars * sources
    pairs = n_row // 2
    assert waves == n_row * LANES
    dims = (n_row, n_col, rows, cols, sources, waves, unknowns)
    vmem = pl.BlockSpec(memory_space=pltpu.VMEM)
    smem = pl.BlockSpec(memory_space=pltpu.SMEM)
    anywhere = pl.BlockSpec(memory_space=pl.ANY)
    dma = pltpu.SemaphoreType.DMA
    bf16, f32 = jnp.bfloat16, jnp.float32
    return pl.pallas_call(
        functools.partial(kernel, dims),
        out_shape=jax.ShapeDtypeStruct((rows, cols, sources, width), f32),
        in_specs=[anywhere, anywhere, smem, smem, vmem, anywhere, vmem],
        out_specs=vmem,
        scratch_shapes=[
            pltpu.VMEM((rows + 2, cols + 2, sources, width), bf16),
            pltpu.VMEM((waves, 2, unknowns), bf16),
            pltpu.VMEM((waves, width), bf16),
            pltpu.VMEM((pairs, 4 * LANES, unknowns), bf16),
            pltpu.VMEM((9, unknowns, 4 * unknowns), bf16),
            pltpu.VMEM((stacked, width), bf16),
            pltpu.VMEM((stacked, 2 * width), bf16),
            pltpu.VMEM((stacked, unknowns), f32),
            pltpu.VMEM((pillars, waves), f32),
            pltpu.VMEM((pillars, waves), f32),
            pltpu.VMEM((n_row, 2 * sources, LANES), PARTIAL),
            pltpu.VMEM((n_row, 2 * sources, LANES), PARTIAL),
            pltpu.VMEM((2 * sources, LANES), f32),
            pltpu.VMEM((n_col, own, LANES), f32),
            pltpu.VMEM((n_col, own, LANES), f32),
            pltpu.VMEM((own, LANES), f32),
            pltpu.VMEM((n_row, n_col, own, LANES), bf16),
            pltpu.VMEM((2, 2 * sources, LANES), f32),
            dma((6,)),
            dma((8,)),
            dma((8,)),
            dma((n_row,)),
            dma((n_row,)),
            dma((n_col,)),
            dma((n_col,)),
            dma((n_col,)),
            dma((n_col,)),
            dma((n_row,)),
            dma((n_row,)),
        ],
        compiler_params=pltpu.CompilerParams(
            collective_id=0, has_side_effects=True, vmem_limit_bytes=56 * 1024 * 1024
        ),
        name="bloch_apply",
    )(
        field,
        near_kernel,
        contact,
        pillar_shift.transpose(0, 2, 1),
        wave_index.T,
        wave_form,
        wave_weight.reshape(waves // LANES, LANES),
    )


def solution(mesh):
    placed = (
        P("row", "col", None, None),
        P(),
        P("row", "col", None),
        P("row", "col", None),
        P(),
        P(),
        P(),
    )
    return jax.shard_map(
        local, mesh=mesh, in_specs=placed, out_specs=P("row", "col", None, None), check_vma=False
    )
```

time: 1010 us -> 50 us (0.05)
  the two profiles are of different devices: /device:TPU:0 before, /device:TPU:1 now
where the time goes in v1:
time: 50 us; the launch traced here: 49.9 us
  Pallas kernels  47.6 us (95%)
  local copies, waits for them, and re-layouts  2.29 us (5%)
    pallas_call x1, Pallas kernels, local(): pl.pallas_call(functools.partial(kernel, dims), out_shape=jax.ShapeDtypeS...  47.6 us
    unnamed x1, local copies, waits for them, and re-layouts  2.29 us

profile of v1, /device:TPU:1, one launch (start us, length us, event | category | flops | bytes accessed | tf_op | source)
XLA Modules:
  0.0 49.9 jit_solution(13342170748258394411)
XLA Ops:
  0.0 47.6 %bloch_apply.1 = f32[4,4,32,512]{3,2,1,0:T(8,128)} custom-call(bf16[4,4,32,512]{3,2,1,0:T(8,128)(2,1)} %field.1, bf16[9,2,2,256,256]{4,3,2,1,0:T(8,128)(2,1)} %near_kernel.1, s32[4,4,9]{2,1,0:T(4,128)} %contact.1, s32[4,2,4]{2,1,0:T(2,128)} %bitcast.5, s32[2,2048]{1,0:T(2,128)} %bitcast.3, bf16[2048,2,256]{2,1,0:T(2,128)(2,1)} %wave_form.1, f32[16,128]{1,0:T(8,128)} %bitcast.4), custom_call_target="tpu_custom_call" | custom-call | tf_op jit(solution)/shard_map/bloch_apply/pallas_call | solution.py:456
  47.6 2.3 %copy.9 = f32[4,4,32,512]{3,2,1,0:T(8,128)} copy(f32[4,4,32,512]{3,2,1,0:T(8,128)} %bloch_apply.1) | data formatting | bytes 2097152

commit v2 on v1

--- a/solution.py
+++ b/solution.py
@@ -16,7 +16,7 @@
 NT = (((1,), (1,)), ((), ()))
 
 PARTIAL = jnp.float32
-NEAR_SPLIT = (0, 3, 5, 7, 9)
+NEAR_SPLIT = (0, 1, 5, 9)
 
 
 def turn_to_cos_sin(turn):
@@ -64,12 +64,8 @@
     sin_all,
     send1,
     recv1,
-    total1,
-    send2,
     recv2,
-    total2,
     waves_in,
-    waves_now,
     local_sem,
     halo_send,
     halo_recv,
@@ -79,14 +75,18 @@
     r2,
     s3,
     r3,
-    s4,
-    r4,
 ):
     n_row, n_col, rows, cols, sources, waves, unknowns = dims
     pillars = rows * cols
-    own = 2 * sources // n_col
+    quarter = 2 * sources // 4
     pairs = n_row // 2
     me_row, me_col = lax.axis_index("row"), lax.axis_index("col")
+    half_cols = n_col // 2
+    inner = [(0, 0), (1, 1), (half_cols, 2), (half_cols + 1, 3)]
+    outer = list(range(2, half_cols, 2))
+    me_q = 2 * lax.div(me_col, half_cols) + lax.rem(me_col, 2)
+    me_slot = 4 * me_row + me_q
+    peers = 4 * n_row - 1
     row_mod, col_mod = Q * rows * n_row, Q * cols * n_col
 
     def at(row_step, col_step):
@@ -111,25 +111,23 @@
 
     barrier = pltpu.get_barrier_semaphore()
 
+    def greet(row, col):
+        pl.semaphore_signal(barrier, inc=1, device_id=(row, col), device_id_type=MESH)
+
     def greet_row(step, _):
-        pl.semaphore_signal(
-            barrier, inc=1, device_id=(lax.rem(me_row + step, n_row), me_col), device_id_type=MESH
-        )
-        return 0
-
-    def greet_col(step, _):
-        pl.semaphore_signal(
-            barrier, inc=1, device_id=(me_row, lax.rem(me_col + step, n_col)), device_id_type=MESH
-        )
-        return 0
-
+        row = lax.rem(me_row + step, n_row)
+        for flip, _q in inner:
+            greet(row, jnp.bitwise_xor(me_col, flip))
+        return 0
+
+    for flip, _q in inner[1:]:
+        greet(me_row, jnp.bitwise_xor(me_col, flip))
     lax.fori_loop(1, n_row, greet_row, 0)
-    lax.fori_loop(1, n_col, greet_col, 0)
-    for row_step in (-1, 1):
-        for col_step in (-1, 1):
-            pl.semaphore_signal(
-                barrier, inc=1, device_id=at(row_step, col_step), device_id_type=MESH
-            )
+    for flip in outer:
+        greet(me_row, jnp.bitwise_xor(me_col, flip))
+    steps = [(a, b) for a in (-1, 0, 1) for b in (-1, 0, 1) if (a, b) != (0, 0)]
+    for row_step, col_step in steps:
+        greet(*at(row_step, col_step))
 
     down = lax.broadcasted_iota(jnp.int32, (pillars, LANES), 0)
     fine_row = jnp.zeros((pillars, LANES), jnp.int32)
@@ -186,46 +184,51 @@
         x2[base + sources : base + 2 * sources, :unknowns] = imag
         x2[base + sources : base + 2 * sources, unknowns:] = real
 
-    pl.semaphore_wait(barrier, (n_row - 1) + (n_col - 1) + 4)
+    pl.semaphore_wait(barrier, peers + len(outer) + len(steps))
 
     halos = []
     spans = {-1: (slice(0, 1), rows + 1), 1: (slice(rows - 1, rows), 0)}
     col_spans = {-1: (slice(0, 1), cols + 1), 1: (slice(cols - 1, cols), 0)}
-    for row_step in (-1, 0, 1):
-        for col_step in (-1, 0, 1):
-            if (row_step, col_step) == (0, 0):
-                continue
-            if row_step:
-                from_row, into = spans[row_step]
-                to_row = slice(into, into + 1)
-            else:
-                from_row, to_row = slice(0, rows), slice(1, rows + 1)
-            if col_step:
-                from_col, into = col_spans[col_step]
-                to_col = slice(into, into + 1)
-            else:
-                from_col, to_col = slice(0, cols), slice(1, cols + 1)
-            k = len(halos)
-            halos.append(
-                pltpu.make_async_remote_copy(
-                    src_ref=field.at[from_row, from_col],
-                    dst_ref=xpad.at[to_row, to_col],
-                    send_sem=halo_send.at[k],
-                    recv_sem=halo_recv.at[k],
-                    device_id=at(row_step, col_step),
-                    device_id_type=MESH,
-                )
+    for row_step, col_step in steps:
+        if row_step:
+            from_row, into = spans[row_step]
+            to_row = slice(into, into + 1)
+        else:
+            from_row, to_row = slice(0, rows), slice(1, rows + 1)
+        if col_step:
+            from_col, into = col_spans[col_step]
+            to_col = slice(into, into + 1)
+        else:
+            from_col, to_col = slice(0, cols), slice(1, cols + 1)
+        k = len(halos)
+        halos.append(
+            pltpu.make_async_remote_copy(
+                src_ref=field.at[from_row, from_col],
+                dst_ref=xpad.at[to_row, to_col],
+                send_sem=halo_send.at[k],
+                recv_sem=halo_recv.at[k],
+                device_id=at(row_step, col_step),
+                device_id_type=MESH,
             )
-    for halo in halos:
-        halo.start()
-
-    def first_copy(peer, slot):
+        )
+
+    def first_copy(row, flip, q):
         return pltpu.make_async_remote_copy(
-            src_ref=send1.at[peer],
-            dst_ref=recv1.at[slot],
-            send_sem=s1.at[peer],
-            recv_sem=r1.at[slot],
-            device_id=(peer, me_col),
+            src_ref=send1.at[4 * row + q],
+            dst_ref=recv1.at[me_slot],
+            send_sem=s1,
+            recv_sem=r1,
+            device_id=(row, jnp.bitwise_xor(me_col, flip)),
+            device_id_type=MESH,
+        )
+
+    def all_first():
+        return pltpu.make_async_remote_copy(
+            src_ref=send1.at[0:peers],
+            dst_ref=recv1.at[0:peers],
+            send_sem=s1,
+            recv_sem=r1,
+            device_id=(me_row, jnp.bitwise_xor(me_col, 1)),
             device_id_type=MESH,
         )
 
@@ -253,19 +256,29 @@
                 s = sin_all[p : p + 1, here]
                 real = real + (c * pr - s * pi)
                 imag = imag + (c * pi + s * pr)
-            peer = 2 * pair + half
-            send1[peer, 0:sources] = real.astype(send1.dtype)
-            send1[peer, sources : 2 * sources] = imag.astype(send1.dtype)
-
-            @pl.when(peer != me_row)
-            def _():
-                first_copy(peer, me_row).start()
+            row = 2 * pair + half
+            for q in range(4):
+                part = (real, imag)[q // 2]
+                low = (q % 2) * quarter
+                send1[4 * row + q] = part[low : low + quarter].astype(send1.dtype)
+            for flip, step_q in inner:
+                if flip:
+                    first_copy(row, flip, jnp.bitwise_xor(me_q, step_q)).start()
+                else:
+
+                    @pl.when(row != me_row)
+                    def _():
+                        first_copy(row, flip, me_q).start()
 
         return 0
 
     lax.fori_loop(0, pairs, project, 0)
-
-    def near_offset(offset, _):
+    recv1[me_slot] = send1[me_slot]
+    for halo in halos:
+        halo.start()
+
+    def near_offset(turn, _):
+        offset = lax.rem(turn + 4, 9)
         a = lax.div(offset, 3)
         b = lax.rem(offset, 3)
         for p in range(pillars):
@@ -290,111 +303,91 @@
 
     for load in loads[2:]:
         load.wait()
+    acc[...] = jnp.zeros_like(acc)
+    lax.fori_loop(NEAR_SPLIT[0], NEAR_SPLIT[1], near_offset, 0)
+
+    all_first().wait_recv()
+
+    def add_row(row, total):
+        for q in range(4):
+            total = total + recv1[4 * row + q].astype(jnp.float32)
+        return total
+
+    recv2[0] = lax.fori_loop(0, n_row, add_row, jnp.zeros((quarter, LANES), jnp.float32))
+
+    seconds = [
+        pltpu.make_async_remote_copy(
+            src_ref=recv2.at[0],
+            dst_ref=recv2.at[1 + k],
+            send_sem=s2.at[k],
+            recv_sem=r2.at[k],
+            device_id=(me_row, jnp.bitwise_xor(me_col, flip)),
+            device_id_type=MESH,
+        )
+        for k, flip in enumerate(outer)
+    ]
+    for second in seconds:
+        second.start()
     for halo in halos:
         halo.wait_recv()
-    acc[...] = jnp.zeros_like(acc)
-    lax.fori_loop(NEAR_SPLIT[0], NEAR_SPLIT[1], near_offset, 0)
-
-    total1[...] = send1[me_row].astype(jnp.float32)
-
-    def gather1(step, _):
-        peer = lax.rem(me_row + step, n_row)
-        first_copy(peer, peer).wait_recv()
-        total1[...] += recv1[peer].astype(jnp.float32)
-        return 0
-
-    lax.fori_loop(1, n_row, gather1, 0)
-    for k in range(n_col):
-        send2[k] = total1[k * own : (k + 1) * own]
-
-    def second_copy(peer, slot):
-        return pltpu.make_async_remote_copy(
-            src_ref=send2.at[peer],
-            dst_ref=recv2.at[slot],
-            send_sem=s2.at[peer],
-            recv_sem=r2.at[slot],
-            device_id=(me_row, peer),
-            device_id_type=MESH,
-        )
-
-    def spread2(step, _):
-        peer = lax.rem(me_col + step, n_col)
-        second_copy(peer, me_col).start()
-        return 0
-
-    lax.fori_loop(1, n_col, spread2, 0)
     lax.fori_loop(NEAR_SPLIT[1], NEAR_SPLIT[2], near_offset, 0)
-
-    total2[...] = send2[me_col]
-
-    def gather2(step, _):
-        peer = lax.rem(me_col + step, n_col)
-        second_copy(peer, peer).wait_recv()
-        total2[...] += recv2[peer]
-        return 0
-
-    lax.fori_loop(1, n_col, gather2, 0)
+    total = recv2[0]
+    for k, second in enumerate(seconds):
+        second.wait_recv()
+        total = total + recv2[1 + k]
+
     far_scale = math.sqrt(unknowns / (waves * rows * n_row * cols * n_col))
     scale = far_scale * wave_weight[pl.ds(me_row, 1), :]
-    waves_in[me_row, me_col] = (scale * total2[...]).astype(jnp.bfloat16)
-
-    def third_copy(peer, slot):
+    waves_in[me_slot] = (scale * total).astype(jnp.bfloat16)
+    my_pair_sem = r3.at[my_pair]
+
+    def third_copy(row, flip):
         return pltpu.make_async_remote_copy(
-            src_ref=waves_in.at[me_row, me_col],
-            dst_ref=waves_in.at[me_row, slot],
-            send_sem=s3.at[peer],
-            recv_sem=r3.at[slot],
-            device_id=(me_row, peer),
+            src_ref=waves_in.at[me_slot],
+            dst_ref=waves_in.at[me_slot],
+            send_sem=s3,
+            recv_sem=my_pair_sem,
+            device_id=(row, jnp.bitwise_xor(me_col, flip)),
             device_id_type=MESH,
         )
 
-    def spread3(step, _):
-        peer = lax.rem(me_col + step, n_col)
-        third_copy(peer, me_col).start()
-        return 0
-
-    lax.fori_loop(1, n_col, spread3, 0)
+    def some_third(first, count, sem):
+        return pltpu.make_async_remote_copy(
+            src_ref=waves_in.at[pl.ds(first, count)],
+            dst_ref=waves_in.at[pl.ds(first, count)],
+            send_sem=s3,
+            recv_sem=sem,
+            device_id=(me_row, jnp.bitwise_xor(me_col, 1)),
+            device_id_type=MESH,
+        )
+
+    def hand_row(step, _):
+        row = lax.rem(me_row + step, n_row)
+        for flip, _q in inner:
+            third_copy(row, flip).start()
+        return 0
+
+    for flip, _q in inner[1:]:
+        third_copy(me_row, flip).start()
+    lax.fori_loop(1, n_row, hand_row, 0)
     lax.fori_loop(NEAR_SPLIT[2], NEAR_SPLIT[3], near_offset, 0)
-
-    def gather3(step, _):
-        peer = lax.rem(me_col + step, n_col)
-        third_copy(peer, peer).wait_recv()
-        return 0
-
-    lax.fori_loop(1, n_col, gather3, 0)
-
-    def fourth_copy(peer, slot):
-        return pltpu.make_async_remote_copy(
-            src_ref=waves_in.at[me_row],
-            dst_ref=waves_in.at[slot],
-            send_sem=s4.at[peer],
-            recv_sem=r4.at[slot],
-            device_id=(peer, me_col),
-            device_id_type=MESH,
-        )
-
-    def spread4(step, _):
-        peer = lax.rem(me_row + step, n_row)
-        fourth_copy(peer, me_row).start()
-        return 0
-
-    lax.fori_loop(1, n_row, spread4, 0)
-    lax.fori_loop(NEAR_SPLIT[3], NEAR_SPLIT[4], near_offset, 0)
 
     def far_pair(step, _):
         pair = lax.rem(my_pair + step, pairs)
+
+        @pl.when(step == 0)
+        def _():
+            some_third(0, 7, my_pair_sem).wait_recv()
+
+        @pl.when(step > 0)
+        def _():
+            some_third(8 * pair, 8, r3.at[pair]).wait_recv()
+
         for half in range(2):
-            peer = 2 * pair + half
-
-            @pl.when(peer != me_row)
-            def _():
-                fourth_copy(peer, peer).wait_recv()
-
-            for k in range(n_col):
-                waves_now[half, k * own : (k + 1) * own] = waves_in[peer, k].astype(jnp.float32)
             here = pl.ds(pl.multiple_of((2 * pair + half) * LANES, LANES), LANES)
-            wr = waves_now[half, 0:sources]
-            wi = waves_now[half, sources : 2 * sources]
+            slot = 4 * (2 * pair + half)
+            wr = waves_in[pl.ds(slot, 2)].reshape(sources, LANES).astype(jnp.float32)
+            wi = waves_in[pl.ds(slot + 2, 2)].reshape(sources, LANES).astype(jnp.float32)
             low = slice(half * LANES, (half + 1) * LANES)
             high = slice((2 + half) * LANES, (3 + half) * LANES)
             for p in range(pillars):
@@ -420,20 +413,10 @@
     for halo in halos:
         halo.wait_send()
 
-    def drain_row(step, _):
-        peer = lax.rem(me_row + step, n_row)
-        first_copy(peer, me_row).wait_send()
-        fourth_copy(peer, me_row).wait_send()
-        return 0
-
-    def drain_col(step, _):
-        peer = lax.rem(me_col + step, n_col)
-        second_copy(peer, me_col).wait_send()
-        third_copy(peer, me_col).wait_send()
-        return 0
-
-    lax.fori_loop(1, n_row, drain_row, 0)
-    lax.fori_loop(1, n_col, drain_col, 0)
+    all_first().wait_send()
+    for second in seconds:
+        second.wait_send()
+    some_third(0, peers, my_pair_sem).wait_send()
 
 
 def local(field, near_kernel, contact, pillar_shift, wave_index, wave_form, wave_weight):
@@ -442,7 +425,7 @@
     unknowns = width // 2
     n_row = lax.axis_size("row")
     n_col = lax.axis_size("col")
-    own = 2 * sources // n_col
+    quarter = 2 * sources // 4
     pillars = rows * cols
     stacked = 2 * pillars * sources
     pairs = n_row // 2
@@ -455,7 +438,7 @@
     bf16, f32 = jnp.bfloat16, jnp.float32
     return pl.pallas_call(
         functools.partial(kernel, dims),
-        out_shape=jax.ShapeDtypeStruct((rows, cols, sources, width), f32),
+        out_shape=pltpu.VMEM((rows, cols, sources, width), f32),
         in_specs=[anywhere, anywhere, smem, smem, vmem, anywhere, vmem],
         out_specs=vmem,
         scratch_shapes=[
@@ -469,25 +452,19 @@
             pltpu.VMEM((stacked, unknowns), f32),
             pltpu.VMEM((pillars, waves), f32),
             pltpu.VMEM((pillars, waves), f32),
-            pltpu.VMEM((n_row, 2 * sources, LANES), PARTIAL),
-            pltpu.VMEM((n_row, 2 * sources, LANES), PARTIAL),
-            pltpu.VMEM((2 * sources, LANES), f32),
-            pltpu.VMEM((n_col, own, LANES), f32),
-            pltpu.VMEM((n_col, own, LANES), f32),
-            pltpu.VMEM((own, LANES), f32),
-            pltpu.VMEM((n_row, n_col, own, LANES), bf16),
-            pltpu.VMEM((2, 2 * sources, LANES), f32),
+            pltpu.VMEM((4 * n_row, quarter, LANES), PARTIAL),
+            pltpu.VMEM((4 * n_row, quarter, LANES), PARTIAL),
+            pltpu.VMEM((max(n_col // 4, 1), quarter, LANES), f32),
+            pltpu.VMEM((4 * n_row, quarter, LANES), bf16),
             dma((6,)),
             dma((8,)),
             dma((8,)),
-            dma((n_row,)),
-            dma((n_row,)),
-            dma((n_col,)),
-            dma((n_col,)),
-            dma((n_col,)),
-            dma((n_col,)),
-            dma((n_row,)),
-            dma((n_row,)),
+            dma,
+            dma,
+            dma((max(n_col // 4 - 1, 1),)),
+            dma((max(n_col // 4 - 1, 1),)),
+            dma,
+            dma((pairs,)),
         ],
         compiler_params=pltpu.CompilerParams(
             collective_id=0, has_side_effects=True, vmem_limit_bytes=56 * 1024 * 1024

time: 50 us -> 41.4 us (0.83)
  Pallas kernels: 47.6 us -> 40.3 us
  local copies, waits for them, and re-layouts: 2.29 us -> 0.97 us
    pallas_call x1, Pallas kernels: 47.6 us -> 40.3 us  [local(): pl.pallas_call(functools.partial(kernel, dims), out_shape=pltpu.VMEM((row...]
    unnamed x1, local copies, waits for them, and re-layouts: 2.29 us -> 0.97 us
where the time goes in v2:
time: 41.4 us; the launch traced here: 41.3 us
  Pallas kernels  40.3 us (97%)
  local copies, waits for them, and re-layouts  0.97 us (2%)
    pallas_call x1, Pallas kernels, local(): pl.pallas_call(functools.partial(kernel, dims), out_shape=pltpu.VMEM((row...  40.3 us
    unnamed x1, local copies, waits for them, and re-layouts  0.97 us

profile of v2, /device:TPU:1, one launch (start us, length us, event | category | flops | bytes accessed | tf_op | source)
XLA Modules:
  0.0 41.3 jit_solution(4798217800274867292)
XLA Ops:
  0.0 40.3 %bloch_apply.1 = f32[4,4,32,512]{3,2,1,0:T(8,128)S(1)} custom-call(bf16[4,4,32,512]{3,2,1,0:T(8,128)(2,1)} %field.1, bf16[9,2,2,256,256]{4,3,2,1,0:T(8,128)(2,1)} %near_kernel.1, s32[4,4,9]{2,1,0:T(4,128)} %contact.1, s32[4,2,4]{2,1,0:T(2,128)} %bitcast.5, s32[2,2048]{1,0:T(2,128)} %bitcast.3, bf16[2048,2,256]{2,1,0:T(2,128)(2,1)} %wave_form.1, ...), custom_call_target="tpu_custom_call" | custom-call | tf_op jit(solution)/shard_map/bloch_apply/pallas_call | solution.py:439
  40.3 1.0 %copy.9 = f32[4,4,32,512]{3,2,1,0:T(8,128)} copy(f32[4,4,32,512]{3,2,1,0:T(8,128)S(1)} %bloch_apply.1) | data formatting | bytes 2097152

commit v3 on v2

--- a/solution.py
+++ b/solution.py
@@ -15,7 +15,7 @@
 MESH = pl.DeviceIdType.MESH
 NT = (((1,), (1,)), ((), ()))
 
-PARTIAL = jnp.float32
+AHEAD = 4
 NEAR_SPLIT = (0, 1, 5, 9)
 
 
@@ -62,6 +62,8 @@
     acc,
     cos_all,
     sin_all,
+    partial,
+    sibling,
     send1,
     recv1,
     recv2,
@@ -69,6 +71,8 @@
     local_sem,
     halo_send,
     halo_recv,
+    s0,
+    r0,
     s1,
     r1,
     s2,
@@ -87,6 +91,9 @@
     me_q = 2 * lax.div(me_col, half_cols) + lax.rem(me_col, 2)
     me_slot = 4 * me_row + me_q
     peers = 4 * n_row - 1
+    my_pair, me_core = lax.div(me_row, 2), lax.rem(me_row, 2)
+    chip_slot = 4 * my_pair + me_q
+    chip_peers = 4 * pairs - 1
     row_mod, col_mod = Q * rows * n_row, Q * cols * n_col
 
     def at(row_step, col_step):
@@ -120,14 +127,15 @@
             greet(row, jnp.bitwise_xor(me_col, flip))
         return 0
 
+    steps = [(a, b) for a in (-1, 0, 1) for b in (-1, 0, 1) if (a, b) != (0, 0)]
+    sideways = [(a, b) for a, b in steps if b]
+    for flip in outer:
+        greet(me_row, jnp.bitwise_xor(me_col, flip))
+    for row_step, col_step in sideways:
+        greet(*at(row_step, col_step))
+    lax.fori_loop(1, n_row, greet_row, 0)
     for flip, _q in inner[1:]:
         greet(me_row, jnp.bitwise_xor(me_col, flip))
-    lax.fori_loop(1, n_row, greet_row, 0)
-    for flip in outer:
-        greet(me_row, jnp.bitwise_xor(me_col, flip))
-    steps = [(a, b) for a in (-1, 0, 1) for b in (-1, 0, 1) if (a, b) != (0, 0)]
-    for row_step, col_step in steps:
-        greet(*at(row_step, col_step))
 
     down = lax.broadcasted_iota(jnp.int32, (pillars, LANES), 0)
     fine_row = jnp.zeros((pillars, LANES), jnp.int32)
@@ -183,8 +191,6 @@
         x2[base : base + sources, unknowns:] = -imag
         x2[base + sources : base + 2 * sources, :unknowns] = imag
         x2[base + sources : base + 2 * sources, unknowns:] = real
-
-    pl.semaphore_wait(barrier, peers + len(outer) + len(steps))
 
     halos = []
     spans = {-1: (slice(0, 1), rows + 1), 1: (slice(rows - 1, rows), 0)}
@@ -212,30 +218,41 @@
             )
         )
 
-    def first_copy(row, flip, q):
+    def sibling_copy(pair):
         return pltpu.make_async_remote_copy(
-            src_ref=send1.at[4 * row + q],
-            dst_ref=recv1.at[me_slot],
+            src_ref=partial.at[pair, 1 - me_core],
+            dst_ref=sibling.at[pair],
+            send_sem=s0.at[pair],
+            recv_sem=r0.at[pair],
+            device_id=(me_row + 1 - 2 * me_core, me_col),
+            device_id_type=MESH,
+        )
+
+    def first_copy(pair, flip, q):
+        return pltpu.make_async_remote_copy(
+            src_ref=send1.at[4 * pair + q],
+            dst_ref=recv1.at[chip_slot],
             send_sem=s1,
             recv_sem=r1,
-            device_id=(row, jnp.bitwise_xor(me_col, flip)),
+            device_id=(2 * pair + me_core, jnp.bitwise_xor(me_col, flip)),
             device_id_type=MESH,
         )
 
     def all_first():
         return pltpu.make_async_remote_copy(
-            src_ref=send1.at[0:peers],
-            dst_ref=recv1.at[0:peers],
+            src_ref=send1.at[0:chip_peers],
+            dst_ref=recv1.at[0:chip_peers],
             send_sem=s1,
             recv_sem=r1,
             device_id=(me_row, jnp.bitwise_xor(me_col, 1)),
             device_id_type=MESH,
         )
 
-    my_pair = lax.div(me_row, 2)
+    def pair_at(step):
+        return lax.rem(my_pair + 1 + step, pairs)
 
     def project(step, _):
-        pair = lax.rem(my_pair + 1 + step, pairs)
+        pair = pair_at(step)
         first = pl.multiple_of(pair * 2 * LANES, 2 * LANES)
         projected = lax.dot_general(
             x2[...],
@@ -256,26 +273,46 @@
                 s = sin_all[p : p + 1, here]
                 real = real + (c * pr - s * pi)
                 imag = imag + (c * pi + s * pr)
-            row = 2 * pair + half
-            for q in range(4):
-                part = (real, imag)[q // 2]
-                low = (q % 2) * quarter
-                send1[4 * row + q] = part[low : low + quarter].astype(send1.dtype)
-            for flip, step_q in inner:
-                if flip:
-                    first_copy(row, flip, jnp.bitwise_xor(me_q, step_q)).start()
-                else:
-
-                    @pl.when(row != me_row)
-                    def _():
-                        first_copy(row, flip, me_q).start()
-
-        return 0
-
-    lax.fori_loop(0, pairs, project, 0)
-    recv1[me_slot] = send1[me_slot]
+            partial[pair, half, :sources] = real
+            partial[pair, half, sources:] = imag
+        return 0
+
+    def give(step, _):
+        sibling_copy(pair_at(step)).start()
+        return 0
+
+    def add_and_send(step, _):
+        pair = pair_at(step)
+        sibling_copy(pair).wait_recv()
+        for q in range(4):
+            span = slice(q * quarter, (q + 1) * quarter)
+            send1[4 * pair + q] = partial[pair, me_core, span] + sibling[pair, span]
+        for flip, step_q in inner:
+            if flip:
+                first_copy(pair, flip, jnp.bitwise_xor(me_q, step_q)).start()
+            else:
+
+                @pl.when(pair != my_pair)
+                def _():
+                    first_copy(pair, flip, me_q).start()
+
+        return 0
+
+    def project_and_send(step, _):
+        project(step, 0)
+        give(step, 0)
+        add_and_send(step - AHEAD, 0)
+        return 0
+
+    ahead = min(AHEAD, pairs)
+    lax.fori_loop(0, ahead, project, 0)
+    pl.semaphore_wait(barrier, peers + len(outer) + len(sideways))
+    lax.fori_loop(0, ahead, give, 0)
     for halo in halos:
         halo.start()
+    lax.fori_loop(ahead, pairs, project_and_send, 0)
+    lax.fori_loop(pairs - ahead, pairs, add_and_send, 0)
+    recv1[chip_slot] = send1[chip_slot]
 
     def near_offset(turn, _):
         offset = lax.rem(turn + 4, 9)
@@ -308,12 +345,12 @@
 
     all_first().wait_recv()
 
-    def add_row(row, total):
+    def add_chip(pair, total):
         for q in range(4):
-            total = total + recv1[4 * row + q].astype(jnp.float32)
+            total = total + recv1[4 * pair + q]
         return total
 
-    recv2[0] = lax.fori_loop(0, n_row, add_row, jnp.zeros((quarter, LANES), jnp.float32))
+    recv2[0] = lax.fori_loop(0, pairs, add_chip, jnp.zeros((quarter, LANES), jnp.float32))
 
     seconds = [
         pltpu.make_async_remote_copy(
@@ -413,6 +450,11 @@
     for halo in halos:
         halo.wait_send()
 
+    def drain(pair, _):
+        sibling_copy(pair).wait_send()
+        return 0
+
+    lax.fori_loop(0, pairs, drain, 0)
     all_first().wait_send()
     for second in seconds:
         second.wait_send()
@@ -452,13 +494,17 @@
             pltpu.VMEM((stacked, unknowns), f32),
             pltpu.VMEM((pillars, waves), f32),
             pltpu.VMEM((pillars, waves), f32),
-            pltpu.VMEM((4 * n_row, quarter, LANES), PARTIAL),
-            pltpu.VMEM((4 * n_row, quarter, LANES), PARTIAL),
+            pltpu.VMEM((pairs, 2, 2 * sources, LANES), f32),
+            pltpu.VMEM((pairs, 2 * sources, LANES), f32),
+            pltpu.VMEM((4 * pairs, quarter, LANES), f32),
+            pltpu.VMEM((4 * pairs, quarter, LANES), f32),
             pltpu.VMEM((max(n_col // 4, 1), quarter, LANES), f32),
             pltpu.VMEM((4 * n_row, quarter, LANES), bf16),
             dma((6,)),
             dma((8,)),
             dma((8,)),
+            dma((pairs,)),
+            dma((pairs,)),
             dma,
             dma,
             dma((max(n_col // 4 - 1, 1),)),

time: 41.4 us -> 39.7 us (0.959)
  Pallas kernels: 40.3 us -> 38.6 us
    pallas_call x1, Pallas kernels: 40.3 us -> 38.6 us  [local(): pl.pallas_call(functools.partial(kernel, dims), out_shape=pltpu.VMEM((row...]
where the time goes in v3:
time: 39.7 us; the launch traced here: 39.5 us
  Pallas kernels  38.6 us (97%)
  local copies, waits for them, and re-layouts  0.97 us (2%)
    pallas_call x1, Pallas kernels, local(): pl.pallas_call(functools.partial(kernel, dims), out_shape=pltpu.VMEM((row...  38.6 us
    unnamed x1, local copies, waits for them, and re-layouts  0.97 us

profile of v3, /device:TPU:1, one launch (start us, length us, event | category | flops | bytes accessed | tf_op | source)
XLA Modules:
  0.0 39.5 jit_solution(1426305643863823130)
XLA Ops:
  0.0 38.6 %bloch_apply.1 = f32[4,4,32,512]{3,2,1,0:T(8,128)S(1)} custom-call(bf16[4,4,32,512]{3,2,1,0:T(8,128)(2,1)} %field.1, bf16[9,2,2,256,256]{4,3,2,1,0:T(8,128)(2,1)} %near_kernel.1, s32[4,4,9]{2,1,0:T(4,128)} %contact.1, s32[4,2,4]{2,1,0:T(2,128)} %bitcast.5, s32[2,2048]{1,0:T(2,128)} %bitcast.3, bf16[2048,2,256]{2,1,0:T(2,128)(2,1)} %wave_form.1, ...), custom_call_target="tpu_custom_call" | custom-call | tf_op jit(solution)/shard_map/bloch_apply/pallas_call | solution.py:481
  38.6 1.0 %copy.9 = f32[4,4,32,512]{3,2,1,0:T(8,128)} copy(f32[4,4,32,512]{3,2,1,0:T(8,128)S(1)} %bloch_apply.1) | data formatting | bytes 2097152

commit v4 on v3

--- a/solution.py
+++ b/solution.py
@@ -16,7 +16,6 @@
 NT = (((1,), (1,)), ((), ()))
 
 AHEAD = 4
-NEAR_SPLIT = (0, 1, 5, 9)
 
 
 def turn_to_cos_sin(turn):
@@ -127,8 +126,8 @@
             greet(row, jnp.bitwise_xor(me_col, flip))
         return 0
 
-    steps = [(a, b) for a in (-1, 0, 1) for b in (-1, 0, 1) if (a, b) != (0, 0)]
-    sideways = [(a, b) for a, b in steps if b]
+    steps = [(0, -1), (0, 1), (-1, 0), (1, 0)]
+    sideways = steps[:2]
     for flip in outer:
         greet(me_row, jnp.bitwise_xor(me_col, flip))
     for row_step, col_step in sideways:
@@ -218,6 +217,22 @@
             )
         )
 
+    corners = []
+    for row_step in (-1, 1):
+        from_row, into = spans[row_step]
+        for edge in (0, cols + 1):
+            k = len(halos) + len(corners)
+            corners.append(
+                pltpu.make_async_remote_copy(
+                    src_ref=xpad.at[1 + from_row.start, edge],
+                    dst_ref=xpad.at[into, edge],
+                    send_sem=halo_send.at[k],
+                    recv_sem=halo_recv.at[k],
+                    device_id=at(row_step, 0),
+                    device_id_type=MESH,
+                )
+            )
+
     def sibling_copy(pair):
         return pltpu.make_async_remote_copy(
             src_ref=partial.at[pair, 1 - me_core],
@@ -314,8 +329,7 @@
     lax.fori_loop(pairs - ahead, pairs, add_and_send, 0)
     recv1[chip_slot] = send1[chip_slot]
 
-    def near_offset(turn, _):
-        offset = lax.rem(turn + 4, 9)
+    def near_offset(offset):
         a = lax.div(offset, 3)
         b = lax.rem(offset, 3)
         for p in range(pillars):
@@ -336,12 +350,19 @@
         acc[...] += lax.dot_general(
             lhs[...], near_mats[offset], NT, preferred_element_type=jnp.float32
         )
+
+    def near_edge(turn, _):
+        near_offset(2 * turn + 1)
+        return 0
+
+    def near_corner(turn, _):
+        near_offset(2 * turn + 2 * lax.div(turn, 2))
         return 0
 
     for load in loads[2:]:
         load.wait()
     acc[...] = jnp.zeros_like(acc)
-    lax.fori_loop(NEAR_SPLIT[0], NEAR_SPLIT[1], near_offset, 0)
+    near_offset(jnp.int32(4))
 
     all_first().wait_recv()
 
@@ -367,7 +388,9 @@
         second.start()
     for halo in halos:
         halo.wait_recv()
-    lax.fori_loop(NEAR_SPLIT[1], NEAR_SPLIT[2], near_offset, 0)
+    for corner in corners:
+        corner.start()
+    lax.fori_loop(0, 4, near_edge, 0)
     total = recv2[0]
     for k, second in enumerate(seconds):
         second.wait_recv()
@@ -407,10 +430,12 @@
     for flip, _q in inner[1:]:
         third_copy(me_row, flip).start()
     lax.fori_loop(1, n_row, hand_row, 0)
-    lax.fori_loop(NEAR_SPLIT[2], NEAR_SPLIT[3], near_offset, 0)
+    for corner in corners:
+        corner.wait_recv()
+    lax.fori_loop(0, 4, near_corner, 0)
 
     def far_pair(step, _):
-        pair = lax.rem(my_pair + step, pairs)
+        pair = lax.rem(my_pair - step + pairs, pairs)
 
         @pl.when(step == 0)
         def _():
@@ -447,7 +472,7 @@
         out[r, c, :, :unknowns] = acc[base : base + sources]
         out[r, c, :, unknowns:] = acc[base + sources : base + 2 * sources]
 
-    for halo in halos:
+    for halo in halos + corners:
         halo.wait_send()
 
     def drain(pair, _):

time: 39.7 us -> 38.1 us (0.960)
  Pallas kernels: 38.6 us -> 37 us
    pallas_call x1, Pallas kernels: 38.6 us -> 37 us  [local(): pl.pallas_call(functools.partial(kernel, dims), out_shape=pltpu.VMEM((row...]
where the time goes in v4:
time: 38.1 us; the launch traced here: 37.9 us
  Pallas kernels  37 us (97%)
  local copies, waits for them, and re-layouts  0.97 us (3%)
    pallas_call x1, Pallas kernels, local(): pl.pallas_call(functools.partial(kernel, dims), out_shape=pltpu.VMEM((row...  37 us
    unnamed x1, local copies, waits for them, and re-layouts  0.97 us

profile of v4, /device:TPU:1, one launch (start us, length us, event | category | flops | bytes accessed | tf_op | source)
XLA Modules:
  0.0 37.9 jit_solution(12489434821205826434)
XLA Ops:
  0.0 37.0 %bloch_apply.1 = f32[4,4,32,512]{3,2,1,0:T(8,128)S(1)} custom-call(bf16[4,4,32,512]{3,2,1,0:T(8,128)(2,1)} %field.1, bf16[9,2,2,256,256]{4,3,2,1,0:T(8,128)(2,1)} %near_kernel.1, s32[4,4,9]{2,1,0:T(4,128)} %contact.1, s32[4,2,4]{2,1,0:T(2,128)} %bitcast.5, s32[2,2048]{1,0:T(2,128)} %bitcast.3, bf16[2048,2,256]{2,1,0:T(2,128)(2,1)} %wave_form.1, ...), custom_call_target="tpu_custom_call" | custom-call | tf_op jit(solution)/shard_map/bloch_apply/pallas_call | solution.py:506
  37.0 1.0 %copy.9 = f32[4,4,32,512]{3,2,1,0:T(8,128)} copy(f32[4,4,32,512]{3,2,1,0:T(8,128)S(1)} %bloch_apply.1) | data formatting | bytes 2097152

commit v5 on v4

--- a/solution.py
+++ b/solution.py
@@ -15,7 +15,7 @@
 MESH = pl.DeviceIdType.MESH
 NT = (((1,), (1,)), ((), ()))
 
-AHEAD = 4
+AHEAD = 2
 
 
 def turn_to_cos_sin(turn):
@@ -81,18 +81,18 @@
 ):
     n_row, n_col, rows, cols, sources, waves, unknowns = dims
     pillars = rows * cols
-    quarter = 2 * sources // 4
+    share = sources
     pairs = n_row // 2
     me_row, me_col = lax.axis_index("row"), lax.axis_index("col")
     half_cols = n_col // 2
-    inner = [(0, 0), (1, 1), (half_cols, 2), (half_cols + 1, 3)]
-    outer = list(range(2, half_cols, 2))
-    me_q = 2 * lax.div(me_col, half_cols) + lax.rem(me_col, 2)
-    me_slot = 4 * me_row + me_q
-    peers = 4 * n_row - 1
+    inner = [(0, 0), (half_cols, 1)]
+    outer = list(range(1, half_cols))
+    me_q = lax.div(me_col, half_cols)
+    me_slot = 2 * me_row + me_q
+    peers = 2 * n_row - 1
     my_pair, me_core = lax.div(me_row, 2), lax.rem(me_row, 2)
-    chip_slot = 4 * my_pair + me_q
-    chip_peers = 4 * pairs - 1
+    chip_slot = 2 * my_pair + me_q
+    chip_peers = 2 * pairs - 1
     row_mod, col_mod = Q * rows * n_row, Q * cols * n_col
 
     def at(row_step, col_step):
@@ -245,7 +245,7 @@
 
     def first_copy(pair, flip, q):
         return pltpu.make_async_remote_copy(
-            src_ref=send1.at[4 * pair + q],
+            src_ref=send1.at[2 * pair + q],
             dst_ref=recv1.at[chip_slot],
             send_sem=s1,
             recv_sem=r1,
@@ -259,7 +259,7 @@
             dst_ref=recv1.at[0:chip_peers],
             send_sem=s1,
             recv_sem=r1,
-            device_id=(me_row, jnp.bitwise_xor(me_col, 1)),
+            device_id=(me_row, jnp.bitwise_xor(me_col, half_cols)),
             device_id_type=MESH,
         )
 
@@ -299,9 +299,9 @@
     def add_and_send(step, _):
         pair = pair_at(step)
         sibling_copy(pair).wait_recv()
-        for q in range(4):
-            span = slice(q * quarter, (q + 1) * quarter)
-            send1[4 * pair + q] = partial[pair, me_core, span] + sibling[pair, span]
+        for q in range(2):
+            span = slice(q * share, (q + 1) * share)
+            send1[2 * pair + q] = partial[pair, me_core, span] + sibling[pair, span]
         for flip, step_q in inner:
             if flip:
                 first_copy(pair, flip, jnp.bitwise_xor(me_q, step_q)).start()
@@ -367,11 +367,11 @@
     all_first().wait_recv()
 
     def add_chip(pair, total):
-        for q in range(4):
-            total = total + recv1[4 * pair + q]
+        for q in range(2):
+            total = total + recv1[2 * pair + q]
         return total
 
-    recv2[0] = lax.fori_loop(0, pairs, add_chip, jnp.zeros((quarter, LANES), jnp.float32))
+    recv2[0] = lax.fori_loop(0, pairs, add_chip, jnp.zeros((share, LANES), jnp.float32))
 
     seconds = [
         pltpu.make_async_remote_copy(
@@ -417,7 +417,7 @@
             dst_ref=waves_in.at[pl.ds(first, count)],
             send_sem=s3,
             recv_sem=sem,
-            device_id=(me_row, jnp.bitwise_xor(me_col, 1)),
+            device_id=(me_row, jnp.bitwise_xor(me_col, half_cols)),
             device_id_type=MESH,
         )
 
@@ -439,17 +439,17 @@
 
         @pl.when(step == 0)
         def _():
-            some_third(0, 7, my_pair_sem).wait_recv()
+            some_third(0, 3, my_pair_sem).wait_recv()
 
         @pl.when(step > 0)
         def _():
-            some_third(8 * pair, 8, r3.at[pair]).wait_recv()
+            some_third(4 * pair, 4, r3.at[pair]).wait_recv()
 
         for half in range(2):
             here = pl.ds(pl.multiple_of((2 * pair + half) * LANES, LANES), LANES)
-            slot = 4 * (2 * pair + half)
-            wr = waves_in[pl.ds(slot, 2)].reshape(sources, LANES).astype(jnp.float32)
-            wi = waves_in[pl.ds(slot + 2, 2)].reshape(sources, LANES).astype(jnp.float32)
+            slot = 2 * (2 * pair + half)
+            wr = waves_in[slot].astype(jnp.float32)
+            wi = waves_in[slot + 1].astype(jnp.float32)
             low = slice(half * LANES, (half + 1) * LANES)
             high = slice((2 + half) * LANES, (3 + half) * LANES)
             for p in range(pillars):
@@ -492,7 +492,7 @@
     unknowns = width // 2
     n_row = lax.axis_size("row")
     n_col = lax.axis_size("col")
-    quarter = 2 * sources // 4
+    share = sources
     pillars = rows * cols
     stacked = 2 * pillars * sources
     pairs = n_row // 2
@@ -521,10 +521,10 @@
             pltpu.VMEM((pillars, waves), f32),
             pltpu.VMEM((pairs, 2, 2 * sources, LANES), f32),
             pltpu.VMEM((pairs, 2 * sources, LANES), f32),
-            pltpu.VMEM((4 * pairs, quarter, LANES), f32),
-            pltpu.VMEM((4 * pairs, quarter, LANES), f32),
-            pltpu.VMEM((max(n_col // 4, 1), quarter, LANES), f32),
-            pltpu.VMEM((4 * n_row, quarter, LANES), bf16),
+            pltpu.VMEM((2 * pairs, share, LANES), f32),
+            pltpu.VMEM((2 * pairs, share, LANES), f32),
+            pltpu.VMEM((n_col // 2, share, LANES), f32),
+            pltpu.VMEM((2 * n_row, share, LANES), bf16),
             dma((6,)),
             dma((8,)),
             dma((8,)),
@@ -532,8 +532,8 @@
             dma((pairs,)),
             dma,
             dma,
-            dma((max(n_col // 4 - 1, 1),)),
-            dma((max(n_col // 4 - 1, 1),)),
+            dma((n_col // 2 - 1,)),
+            dma((n_col // 2 - 1,)),
             dma,
             dma((pairs,)),
         ],

time: 38.1 us -> 37.5 us (0.984)
  Pallas kernels: 37 us -> 36.3 us
    pallas_call x1, Pallas kernels: 37 us -> 36.3 us  [local(): pl.pallas_call(functools.partial(kernel, dims), out_shape=pltpu.VMEM((row...]
where the time goes in v5:
time: 37.5 us; the launch traced here: 37.3 us
  Pallas kernels  36.3 us (97%)
  local copies, waits for them, and re-layouts  0.97 us (3%)
    pallas_call x1, Pallas kernels, local(): pl.pallas_call(functools.partial(kernel, dims), out_shape=pltpu.VMEM((row...  36.3 us
    unnamed x1, local copies, waits for them, and re-layouts  0.97 us

profile of v5, /device:TPU:1, one launch (start us, length us, event | category | flops | bytes accessed | tf_op | source)
XLA Modules:
  0.0 37.3 jit_solution(15032874528787994136)
XLA Ops:
  0.0 36.3 %bloch_apply.1 = f32[4,4,32,512]{3,2,1,0:T(8,128)S(1)} custom-call(bf16[4,4,32,512]{3,2,1,0:T(8,128)(2,1)} %field.1, bf16[9,2,2,256,256]{4,3,2,1,0:T(8,128)(2,1)} %near_kernel.1, s32[4,4,9]{2,1,0:T(4,128)} %contact.1, s32[4,2,4]{2,1,0:T(2,128)} %bitcast.5, s32[2,2048]{1,0:T(2,128)} %bitcast.3, bf16[2048,2,256]{2,1,0:T(2,128)(2,1)} %wave_form.1, ...), custom_call_target="tpu_custom_call" | custom-call | tf_op jit(solution)/shard_map/bloch_apply/pallas_call | solution.py:506
  36.3 1.0 %copy.9 = f32[4,4,32,512]{3,2,1,0:T(8,128)} copy(f32[4,4,32,512]{3,2,1,0:T(8,128)S(1)} %bloch_apply.1) | data formatting | bytes 2097152

commit v6 on v5

--- a/solution.py
+++ b/solution.py
@@ -86,7 +86,7 @@
     me_row, me_col = lax.axis_index("row"), lax.axis_index("col")
     half_cols = n_col // 2
     inner = [(0, 0), (half_cols, 1)]
-    outer = list(range(1, half_cols))
+    outer = sorted(range(1, half_cols), key=lambda flip: -min(flip, half_cols - flip))
     me_q = lax.div(me_col, half_cols)
     me_slot = 2 * me_row + me_q
     peers = 2 * n_row - 1

time: 37.5 us -> 36.7 us (0.979)
  Pallas kernels: 36.3 us -> 35.6 us
    pallas_call x1, Pallas kernels: 36.3 us -> 35.6 us  [local(): pl.pallas_call(functools.partial(kernel, dims), out_shape=pltpu.VMEM((row...]
where the time goes in v6:
time: 36.7 us; the launch traced here: 36.5 us
  Pallas kernels  35.6 us (97%)
  local copies, waits for them, and re-layouts  0.97 us (3%)
    pallas_call x1, Pallas kernels, local(): pl.pallas_call(functools.partial(kernel, dims), out_shape=pltpu.VMEM((row...  35.6 us
    unnamed x1, local copies, waits for them, and re-layouts  0.97 us

profile of v6, /device:TPU:1, one launch (start us, length us, event | category | flops | bytes accessed | tf_op | source)
XLA Modules:
  0.0 36.5 jit_solution(17996201261402436465)
XLA Ops:
  0.0 35.6 %bloch_apply.1 = f32[4,4,32,512]{3,2,1,0:T(8,128)S(1)} custom-call(bf16[4,4,32,512]{3,2,1,0:T(8,128)(2,1)} %field.1, bf16[9,2,2,256,256]{4,3,2,1,0:T(8,128)(2,1)} %near_kernel.1, s32[4,4,9]{2,1,0:T(4,128)} %contact.1, s32[4,2,4]{2,1,0:T(2,128)} %bitcast.5, s32[2,2048]{1,0:T(2,128)} %bitcast.3, bf16[2048,2,256]{2,1,0:T(2,128)(2,1)} %wave_form.1, ...), custom_call_target="tpu_custom_call" | custom-call | tf_op jit(solution)/shard_map/bloch_apply/pallas_call | solution.py:506
  35.6 1.0 %copy.9 = f32[4,4,32,512]{3,2,1,0:T(8,128)} copy(f32[4,4,32,512]{3,2,1,0:T(8,128)S(1)} %bloch_apply.1) | data formatting | bytes 2097152
